TPU v7x, 128 devices: a whole 4x4x4 slice. The times are simulated.
128 devices in a mesh: rows: 8 (over x, z_lo), cols: 16 (over z_hi, y, core).
Axes of the slice: x: 4, y: 4, z: 4 (z_hi: 2, z_lo: 2; z = z_hi * 2 + z_lo), core: 2. Of those that a mesh axis runs over, the one named last changes fastest.
Arguments:
- ancestor_inv: bfloat16 [16384, 16384], P('rows', 'cols'), may hold values from -0.0625 to 0.0625
- lfactor: bfloat16 [32, 256, 6, 256], P('cols'), may hold values from -0.8984375 to 0.8984375
- struct: int32 [6, 32], replicated, may hold values from 0 to 63, as said below
- validity: int32 [6, 32], replicated, may hold values from 0 to 1, as said below
- diag_inverse: float32 [6, 256, 256], replicated, may hold values from -6 to 6
Outputs:
- column_block: bfloat16 [16384, 1536], P(('rows', 'cols'))
- diagonal_block: float32 [6, 256, 256], replicated
Inputs may be any that keep to these rules, and one draw needn't show every extreme that they name: `struct`: within a supernode the 32 tile indices are distinct and increasing, and every list holds tiles 0 and 63. `validity`: every tile index of 0 to 63 is a valid entry of some supernode's list; some supernode has all 32 flags set.
All inputs are finite; a program needn't handle non-finite values.
Results may differ from a plain program's by a relative error of at most 0.001.
Values may be sent and summed in bfloat16 or wider, within the bound.
No kernel may reach another device: no remote copies, remote signals or barrier semaphores. Data moves between devices by JAX's collectives and lax.ppermute only.
A program may use at most 192 MiB of HBM per device.

v0:
```python
import functools

import jax
import jax.numpy as jnp
from jax import lax
from jax.experimental import pallas as pl
from jax.experimental.pallas import tpu as pltpu
from jax.sharding import Mesh, PartitionSpec as P


BF16 = jnp.bfloat16
F32 = jnp.float32
I16 = jnp.int16
NX, NL, NH, NY, NC = 4, 2, 2, 4, 2
XL = ("x", "l")
HY = ("h", "y")
CHIPS = XL + HY
CORE_SWAP = [(0, 1), (1, 0)]
UP = [(i, (i + 1) % NX) for i in range(NX)]
DOWN = [(i, (i - 1) % NX) for i in range(NX)]
LEVELS = 32000.0
LOWEST = -100.0
LANES = 128


def level_of(top):
    return jnp.maximum(jnp.ceil(jnp.log2(jnp.maximum(top, 1e-37)) + 0.01), LOWEST)


def code(values, level):
    return jnp.round(values * (jnp.exp2(-level) * LEVELS)).astype(jnp.int32).astype(I16)


def plain(coded):
    return coded.astype(jnp.int32).astype(F32)


def scale_of(level):
    return jnp.exp2(level) * (1.0 / LEVELS)


def share_kernel(where, l_ref, o_ref, buffer, sem):
    part = o_ref.shape[3]
    copy = pltpu.make_async_copy(
        l_ref.at[:, :, pl.ds(pl.multiple_of(where[2] * part, part), part)], buffer, sem
    )
    copy.start()
    copy.wait()
    members = o_ref.shape[2]
    for i in range(o_ref.shape[0]):
        core = i % NC
        o_ref[i] = buffer[:, core * members : (core + 1) * members]


def stage_kernel(where, own_ref, other_ref, near_ref, below_ref, o_ref, parts_ref, sems):
    core = where[1]
    copies = [
        pltpu.make_async_copy(own_ref, o_ref.at[core], sems.at[0]),
        pltpu.make_async_copy(other_ref, o_ref.at[1 - core], sems.at[1]),
        pltpu.make_async_copy(near_ref, parts_ref.at[0], sems.at[2]),
        pltpu.make_async_copy(below_ref, parts_ref.at[1], sems.at[3]),
    ]
    for copy in copies:
        copy.start()
    for copy in copies:
        copy.wait()


def pick_kernel(place, where, x_ref, window_ref, own_ref):
    members, window = window_ref.shape[:2]
    groups = own_ref.shape[0]
    chip, core = where[0], where[1]
    for k in range(members):

        def tile(t):
            p = place[core * members + k, t]
            block = x_ref[jnp.maximum(p, 0), k]
            return jnp.where(p >= 0, block, jnp.zeros_like(block))

        for s in range(window):
            window_ref[k, s] = tile(chip * window + s)
        for g in range(groups):
            own_ref[g, k] = tile(g * window + chip)


def list_window(place, where, order):
    members, window = order.shape[0], order.shape[1] - 1
    chip, core = where[0], where[1]
    for k in range(members):
        listed = [place[core * members + k, chip * window + s] >= 0 for s in range(window)]
        count = sum(jnp.where(f, 1, 0) for f in listed)
        order[k, window] = count
        front, back = jnp.int32(0), count
        for s in range(window):
            order[k, jnp.where(listed[s], front, back)] = s
            front = front + jnp.where(listed[s], 1, 0)
            back = back + jnp.where(listed[s], 0, 1)


def first_kernel(shifts, place, where, a_ref, first_parts, *refs):
    inputs = NL * NX - 2
    parts, outs = refs[:inputs], refs[inputs : inputs + len(shifts)]
    panel, order, sems = refs[inputs + len(shifts) :]
    x, l = where[3], where[4]

    @pl.when(pl.program_id(0) == 0)
    def _():
        copies = []
        for side in range(NL):
            for hop, shift in enumerate(RING):
                source = lax.rem(x + shift, NX) * NL + lax.rem(l + side, NL)
                i = side * NX + hop
                part = first_parts.at[i] if i < 2 else parts[i - 2]
                copies.append(pltpu.make_async_copy(part, panel.at[:, :, source], sems.at[i]))
        for copy in copies:
            copy.start()
        list_window(place, where, order)
        for copy in copies:
            copy.wait()

    products(shifts, place, where, a_ref, panel, order, outs)


def second_kernel(shifts, place, where, a_ref, panel, *refs):
    outs, order = refs[:-1], refs[-1]

    @pl.when(pl.program_id(0) == 0)
    def _():
        list_window(place, where, order)

    products(shifts, place, where, a_ref, panel, order, outs)


def products(shifts, place, where, a_ref, panel, order, outs):
    members, window, _, _, size = panel.shape
    half = window // NC
    core, group, h, y = where[1], where[2], where[5], where[6]
    step = pl.program_id(0)
    j = step + shifts[0]
    tile = group * window + lax.rem(h + lax.div(j, NY), NH) * NY + lax.rem(y + j, NY)

    for k in range(members):
        cols = slice(k * size, (k + 1) * size)
        wanted = place[core * members + k, tile] >= 0
        few = order[k, window] <= half

        def store(values):
            for i, out in enumerate(outs):

                @pl.when(step == i)
                def _():
                    out[:, cols] = values

        def finish(tiles):
            values = jnp.zeros((size, size), F32)
            for s in tiles:
                start = pl.multiple_of(lax.rem(s, half) * size, size)
                left = a_ref[lax.div(s, half), :, pl.ds(start, size)]
                values += jnp.dot(left, panel[k, s].reshape(size, size), preferred_element_type=F32)
            level = level_of(jnp.max(jnp.abs(values), axis=0, keepdims=True))
            tail = jnp.broadcast_to(level, (16, size)).astype(jnp.int32).astype(I16)
            store(jnp.concatenate([code(values, level), tail], axis=0))

        @pl.when(jnp.logical_and(wanted, few))
        def _():
            finish([order[k, i] for i in range(half)])

        @pl.when(jnp.logical_and(wanted, jnp.logical_not(few)))
        def _():
            finish([jnp.int32(s) for s in range(window)])

        @pl.when(jnp.logical_not(wanted))
        def _():
            store(jnp.zeros((size + 16, size), I16))


def diagonal_kernel(place, where, *refs):
    count = NH * NY
    coded, parts, (d_ref, block) = refs[:count], refs[count : 2 * count], refs[2 * count :]
    _, members, _, size = parts[0].shape
    core, group, h, y = where[1], where[2], where[5], where[6]
    block[...] = jnp.zeros_like(block)
    for side in range(NH):
        for hop, shift in enumerate(RING):
            tile = lax.rem(h + side, NH) * NY + lax.rem(y + shift, NY)
            q_ref, ref = coded[side * NY + shift], parts[side * NY + hop]
            for k in range(members):
                cols = slice(k * size, (k + 1) * size)

                @pl.when(place[core * members + k, group * count + tile] >= 0)
                def _():
                    own = ref[:, k].reshape(size, size)
                    rest = plain(q_ref[:size, cols])
                    high = rest.astype(BF16)
                    low = (rest - high.astype(F32)).astype(BF16)
                    total = sum(
                        lax.dot_general(
                            own, term, (((0,), (0,)), ((), ())), preferred_element_type=F32
                        )
                        for term in (high, low)
                    )
                    block[:, cols] -= total * scale_of(plain(q_ref[size : size + 16, cols])[:1])

    values = block[...]
    level = level_of(jnp.max(jnp.abs(values), keepdims=True))
    width = values.shape[1] // 2
    for i in range(2):
        d_ref[i, :, :width] = code(values[:, i * width : (i + 1) * width], level)
        d_ref[i, :, width:] = jnp.broadcast_to(level, (size, LANES)).astype(jnp.int32).astype(I16)


def finish_kernel(place, where, *refs):
    parts, (u_ref, swap_ref) = refs[:-2], refs[-2:]
    sources = len(parts)
    slab, width = u_ref.shape
    size = 2 * slab
    members = width // size
    chip, core, group = where[0], where[1], where[2]
    mine = group * sources + chip
    for k in range(members):
        cols = slice(k * size, (k + 1) * size)
        total = jnp.zeros((size, size), F32)
        for ref in parts:
            scale = scale_of(plain(ref[size : size + 16, cols])[:1])
            total += plain(ref[:size, cols]) * scale
        keep = place[core * members + k, mine] >= 0
        rounded = jnp.where(keep, -total, jnp.zeros_like(total)).astype(BF16)
        first = core == 0
        u_ref[:, cols] = jnp.where(first, rounded[:slab], rounded[slab:])
        swap_ref[:, cols] = jnp.where(first, rounded[slab:], rounded[:slab])


def piece_kernel(q_ref, inverse_ref, o_ref):
    width = q_ref.shape[2] - LANES
    scale = scale_of(plain(q_ref[:, :, width:]))
    sums = [
        jnp.sum(plain(q_ref[:, :, i : i + LANES]) * scale, axis=0) for i in range(0, width, LANES)
    ]
    values = inverse_ref[...] - jnp.concatenate(sums, axis=1)
    level = level_of(jnp.max(jnp.abs(values), keepdims=True))
    coded = jnp.concatenate(
        [
            code(values, level),
            jnp.broadcast_to(level, (values.shape[0], LANES)).astype(jnp.int32).astype(I16),
        ],
        axis=1,
    )
    for j in range(o_ref.shape[0]):
        o_ref[j] = coded


def total_kernel(q_ref, o_ref):
    pieces, cores, depth, reach = q_ref.shape
    supers, size, _ = o_ref.shape
    width = reach - LANES
    count = pieces // 2
    for c in range(cores):
        for i in range(2):
            rows = slice(i * count, (i + 1) * count)
            scale = scale_of(plain(q_ref[rows, c, :, width:]))
            for t in range(width // LANES):
                lane = (i * width + t * LANES) % size
                k = c * (supers // cores) + (i * width + t * LANES) // size
                values = plain(q_ref[rows, c, :, t * LANES : (t + 1) * LANES]) * scale
                o_ref[k, :, lane : lane + LANES] = values.reshape(count * depth, LANES)


def spread(own, axis, up):
    below = lax.ppermute(own, axis, UP)
    above = lax.ppermute(own, axis, DOWN)
    far = lax.ppermute(below, axis, UP) if up else lax.ppermute(above, axis, DOWN)
    return [own, below, above, far]


RING = (0, 3, 1, 2)


def update(ancestor_inv, lfactor, struct, validity, diag_inverse):
    rows, cols = ancestor_inv.shape
    entries, size, supers, _ = lfactor.shape
    groups = NX * NL
    chips = NH * NY
    part = size // groups
    members = supers // NC
    width = members * size
    group = lax.axis_index(XL)
    chip = lax.axis_index(HY)
    core = lax.axis_index("c")
    listed = struct.shape[1]
    tiles = rows * groups // size
    window = tiles // chips
    smem = pl.BlockSpec(memory_space=pltpu.SMEM)
    vmem = pl.BlockSpec(memory_space=pltpu.VMEM)

    other = lax.ppermute(ancestor_inv, "c", CORE_SWAP)

    hits = (struct[:, :, None] == jnp.arange(tiles, dtype=jnp.int32)) & (validity[:, :, None] > 0)
    position = jnp.arange(listed, dtype=jnp.int32)[None, :, None]
    place = jnp.max(jnp.where(hits, position, -1), axis=1)
    where = jnp.stack([chip, core, group] + [lax.axis_index(a) for a in ("x", "l", "h", "y")])

    share = pl.pallas_call(
        share_kernel,
        out_shape=jax.ShapeDtypeStruct((chips * NC, entries, members, part, size), BF16),
        in_specs=[smem, pl.BlockSpec(memory_space=pltpu.HBM)],
        out_specs=vmem,
        scratch_shapes=[
            pltpu.VMEM((entries, supers, part, size), BF16),
            pltpu.SemaphoreType.DMA,
        ],
        name="share",
    )(where, jnp.transpose(lfactor, (0, 2, 1, 3)))
    share = lax.all_to_all(share, ("h", "y", "c"), split_axis=0, concat_axis=0, tiled=True)
    share = share.reshape(listed, members, part, size)

    block = jax.ShapeDtypeStruct((members, window, part, size), BF16)
    near, own = pl.pallas_call(
        pick_kernel,
        out_shape=[block, jax.ShapeDtypeStruct((groups, members, part, size), BF16)],
        in_specs=[smem, smem, vmem],
        out_specs=[vmem] * 2,
        compiler_params=pltpu.CompilerParams(vmem_limit_bytes=8 << 20),
        name="pick",
    )(place, where, share)
    across = lax.ppermute(near, "l", CORE_SWAP)
    window_parts = spread(near, "x", True)
    window_parts += spread(across, "x", False)
    own = lax.all_to_all(own, XL, split_axis=0, concat_axis=0, tiled=True)
    across = lax.ppermute(own, "h", CORE_SWAP)
    row_parts = spread(own, "y", True)
    row_parts += spread(across, "y", False)

    anywhere = pl.BlockSpec(memory_space=pl.ANY)
    staged, first_parts = pl.pallas_call(
        stage_kernel,
        out_shape=[
            jax.ShapeDtypeStruct((NC, rows, cols), BF16),
            jax.ShapeDtypeStruct((2, members, window, part, size), BF16),
        ],
        in_specs=[smem] + [anywhere] * 4,
        out_specs=[anywhere] * 2,
        scratch_shapes=[pltpu.SemaphoreType.DMA((4,))],
        compiler_params=pltpu.CompilerParams(vmem_limit_bytes=1 << 20),
        name="stage",
    )(where, ancestor_inv, other, *window_parts[:2])

    def row_tile(shifts):
        def index(i, _, where):
            j = i + shifts[0]
            tile = lax.rem(where[5] + lax.div(j, NY), NH) * NY + lax.rem(where[6] + j, NY)
            return 0, tile, 0

        return pl.BlockSpec((NC, size, cols), index)

    panel = jax.ShapeDtypeStruct((members, window, groups, part, size), BF16)
    block = jax.ShapeDtypeStruct((size + 16, width), I16)
    order = pltpu.SMEM((members, window + 1), jnp.int32)
    params = pltpu.CompilerParams(vmem_limit_bytes=20 << 20)
    late, early = tuple(range(5)), tuple(range(5, chips))
    *coded_early, panel = pl.pallas_call(
        functools.partial(first_kernel, early),
        out_shape=[block] * len(early) + [panel],
        grid_spec=pltpu.PrefetchScalarGridSpec(
            num_scalar_prefetch=2,
            grid=(len(early),),
            in_specs=[row_tile(early)] + [anywhere] * (len(window_parts) - 1),
            out_specs=[vmem] * (len(early) + 1),
            scratch_shapes=[order, pltpu.SemaphoreType.DMA((len(window_parts),))],
        ),
        compiler_params=params,
        name="first",
    )(place, where, staged, first_parts, *window_parts[2:])
    coded = pl.pallas_call(
        functools.partial(second_kernel, late),
        out_shape=[block] * len(late),
        grid_spec=pltpu.PrefetchScalarGridSpec(
            num_scalar_prefetch=2,
            grid=(len(late),),
            in_specs=[row_tile(late), vmem],
            out_specs=[vmem] * len(late),
            scratch_shapes=[order],
        ),
        compiler_params=params,
        name="second",
    )(place, where, staged, panel)
    coded = list(coded) + list(coded_early)

    pieces = groups * chips

    depth = 2 * size // pieces
    reach = width // 2 + LANES
    diag = pl.pallas_call(
        diagonal_kernel,
        out_shape=jax.ShapeDtypeStruct((2, size, reach), I16),
        in_specs=[smem, smem] + [vmem] * (chips + len(row_parts)),
        out_specs=vmem,
        scratch_shapes=[pltpu.VMEM((size, width), F32)],
        compiler_params=pltpu.CompilerParams(vmem_limit_bytes=16 << 20),
        name="diagonal",
    )(place, where, *coded, *row_parts)

    sums = [coded[0]]
    for shifts in ((6, 5, 7), (4, 2), (1, 3)):
        for j in shifts:
            to = [
                (h * NY + y, (h + j // NY) % NH * NY + (y + j) % NY)
                for h in range(NH)
                for y in range(NY)
            ]
            sums.append(lax.ppermute(coded[j], HY, to))
    slab = jax.ShapeDtypeStruct((size // NC, width), BF16)
    mine, theirs = pl.pallas_call(
        finish_kernel,
        out_shape=[slab, slab],
        in_specs=[smem, smem] + [vmem] * len(sums),
        out_specs=[vmem] * 2,
        compiler_params=pltpu.CompilerParams(vmem_limit_bytes=12 << 20),
        name="finish",
    )(place, where, *sums)

    theirs = lax.ppermute(theirs, "c", CORE_SWAP)
    column_block = jnp.where(
        core == 0,
        jnp.concatenate([mine, theirs], axis=1),
        jnp.concatenate([theirs, mine], axis=1),
    )

    diag = diag.reshape(pieces, depth, reach)
    diag = lax.all_to_all(diag, CHIPS, split_axis=0, concat_axis=0, tiled=True)
    index = group * chips + chip
    inverse = lax.dynamic_slice(
        diag_inverse,
        (core * members, index % (pieces // 2) * depth, 0),
        (members, depth, size),
    )
    inverse = jnp.transpose(inverse, (1, 0, 2)).reshape(depth, 2, width // 2)
    inverse = lax.dynamic_index_in_dim(inverse, index // (pieces // 2), 1, keepdims=False)
    piece = pl.pallas_call(
        piece_kernel,
        out_shape=jax.ShapeDtypeStruct((pieces * NC, depth, reach), I16),
        in_specs=[vmem, vmem],
        out_specs=vmem,
        compiler_params=pltpu.CompilerParams(vmem_limit_bytes=6 << 20),
        name="piece",
    )(diag, inverse)
    whole = lax.all_to_all(piece, CHIPS + ("c",), split_axis=0, concat_axis=0, tiled=True)
    diagonal = pl.pallas_call(
        total_kernel,
        out_shape=jax.ShapeDtypeStruct(diag_inverse.shape, F32),
        in_specs=[vmem],
        out_specs=vmem,
        compiler_params=pltpu.CompilerParams(vmem_limit_bytes=12 << 20),
        name="total",
    )(whole.reshape(pieces, NC, depth, reach))
    return column_block, diagonal


def solution(mesh):
    fine = Mesh(mesh.devices.reshape(NX, NL, NH, NY, NC), ("x", "l", "h", "y", "c"))
    return jax.shard_map(
        update,
        mesh=fine,
        in_specs=(P(XL, ("h", "y", "c")), P(("h", "y", "c")), P(), P(), P()),
        out_specs=(P(("x", "l", "h", "y", "c")), P()),
        check_vma=False,
    )
```

profile of v0, /device:TPU:15, one launch (start us, length us, event | category | flops | bytes accessed | tf_op | source)
XLA Modules:
  0.0 202.4 jit_solution(2374289316279648868)
XLA Ops:
  0.6 0.8 collective-permute-start
  1.4 0.7 stack.31.where
  2.1 2.8 %share.1 = bf16[16,2,3,32,256]{4,3,2,1,0:T(8,128)(2,1)} custom-call(s32[7]{0:T(128)} %stack.31.where, bf16[2,6,256,256]{3,2,1,0:T(8,128)(2,1)} %bitcast.18), custom_call_target="tpu_custom_call" | custom-call | tf_op jit(solution)/shard_map/share/pallas_call | solution.py:302
  4.9 8.0 %all-to-all-start = ((bf16[16,2,3,32,256]{4,3,2,1,0:T(8,128)(2,1)}), bf16[16,2,3,32,256]{4,3,2,1,0:T(8,128)(2,1)S(1)}, u32[]{:S(2)}, u32[]{:S(2)}) async-start(bf16[16,2,3,32,256]{4,3,2,1,0:T(8,128)(2,1)} %share.1), calls=%async_computation | async-start | bytes 3145728 | tf_op jit(solution)/shard_map/all_to_all | solution.py:313
  13.1 20.8 %all-to-all-done = bf16[16,2,3,32,256]{4,3,2,1,0:T(8,128)(2,1)S(1)} async-done(((bf16[16,2,3,32,256]{4,3,2,1,0:T(8,128)(2,1)}), bf16[16,2,3,32,256]{4,3,2,1,0:T(8,128)(2,1)S(1)}, u32[]{:S(2)}, u32[]{:S(2)}) %all-to-all-start) | async-done | bytes 1572896 | tf_op jit(solution)/shard_map/all_to_all | solution.py:313
  33.9 0.8 pick.1
  34.7 0.7 copy-done.9
  35.7 5.4 %all-to-all-start.1 = ((bf16[8,3,32,256]{3,2,1,0:T(8,128)(2,1)}), bf16[8,3,32,256]{3,2,1,0:T(8,128)(2,1)S(1)}, u32[]{:S(2)}, u32[]{:S(2)}) async-start(bf16[8,3,32,256]{3,2,1,0:T(8,128)(2,1)} %copy-done.9), calls=%async_computation.1 | async-start | bytes 786432 | tf_op jit(solution)/shard_map/all_to_all | solution.py:328
  41.1 1.2 collective-permute-start.4
  42.3 0.6 collective-permute-start.2
  42.8 6.5 %all-to-all-done.1.refs_8_ = bf16[8,3,32,256]{3,2,1,0:T(8,128)(2,1)S(1)} async-done(((bf16[8,3,32,256]{3,2,1,0:T(8,128)(2,1)}), bf16[8,3,32,256]{3,2,1,0:T(8,128)(2,1)S(1)}, u32[]{:S(2)}, u32[]{:S(2)}) %all-to-all-start.1) | async-done | bytes 393248 | tf_op jit(solution)/shard_map/all_to_all | solution.py:328
  49.3 2.1 %collective-permute-start.19 = (bf16[8,3,32,256]{3,2,1,0:T(8,128)(2,1)S(1)}, bf16[8,3,32,256]{3,2,1,0:T(8,128)(2,1)S(1)}, u32[]{:S(2)}, u32[]{:S(2)}) collective-permute-start(bf16[8,3,32,256]{3,2,1,0:T(8,128)(2,1)S(1)} %all-to-all-done.1.refs_8_), channel_id=1, source_target_pairs={{0,8},{8,0},{1,9},{9,1},{2,10},{10,2},{3,11},{11,3},{4,12},{12,4},... | collective-permute-start | bytes 1179656 | tf_op jit(solution)/shard_map/ppermute | solution.py:329
  51.4 1.3 collective-permute-start.16
  52.8 3.1 %collective-permute-done.4.refs_2_ = bf16[3,8,32,256]{3,2,1,0:T(8,128)(2,1)S(1)} collective-permute-done((bf16[3,8,32,256]{3,2,1,0:T(8,128)(2,1)S(1)}, bf16[3,8,32,256]{3,2,1,0:T(8,128)(2,1)S(1)}, u32[]{:S(2)}, u32[]{:S(2)}) %collective-permute-start.4) | collective-permute-done | bytes 393248 | tf_op jit(solution)/shard_map/ppermute | solution.py:325
  55.8 2.7 %collective-permute-start.5 = (bf16[3,8,32,256]{3,2,1,0:T(8,128)(2,1)S(1)}, bf16[3,8,32,256]{3,2,1,0:T(8,128)(2,1)S(1)}, u32[]{:S(2)}, u32[]{:S(2)}) collective-permute-start(bf16[3,8,32,256]{3,2,1,0:T(8,128)(2,1)S(1)} %collective-permute-done.4.refs_2_), channel_id=1, source_target_pairs={{0,32},{32,64},{64,96},{96,0},{1,33},{33,65},{65,97},{97,1},{2,34}... | collective-permute-start | bytes 1179656 | tf_op jit(solution)/shard_map/ppermute | solution.py:269
  58.5 6.5 %collective-permute-done.19.refs_12_ = bf16[8,3,32,256]{3,2,1,0:T(8,128)(2,1)S(1)} collective-permute-done((bf16[8,3,32,256]{3,2,1,0:T(8,128)(2,1)S(1)}, bf16[8,3,32,256]{3,2,1,0:T(8,128)(2,1)S(1)}, u32[]{:S(2)}, u32[]{:S(2)}) %collective-permute-start.19) | collective-permute-done | bytes 393248 | tf_op jit(solution)/shard_map/ppermute | solution.py:329
  65.0 0.7 collective-permute-start.3
  65.7 0.4 collective-permute-start.21
  66.2 1.4 collective-permute-start.7
  67.5 0.7 collective-permute-start.17
  68.2 6.4 %collective-permute-done.3.refs_1_ = bf16[3,8,32,256]{3,2,1,0:T(8,128)(2,1)S(1)} collective-permute-done((bf16[3,8,32,256]{3,2,1,0:T(8,128)(2,1)S(1)}, bf16[3,8,32,256]{3,2,1,0:T(8,128)(2,1)S(1)}, u32[]{:S(2)}, u32[]{:S(2)}) %collective-permute-start.3) | collective-permute-done | bytes 393248 | tf_op jit(solution)/shard_map/ppermute | solution.py:271
  74.6 0.9 collective-permute-start.20
  75.5 1.7 collective-permute-start.18
  77.3 2.2 %copy-done.1 = bf16[2048,1024]{1,0:T(8,128)(2,1)S(1)} copy-done((bf16[2048,1024]{1,0:T(8,128)(2,1)S(1)}, bf16[2048,1024]{1,0:T(8,128)(2,1)}, u32[]{:S(2)}) %copy-start.1) | copy-done | bytes 4194328
  79.5 3.0 %stage.1 = (bf16[2,2048,1024]{2,1,0:T(8,128)(2,1)S(1)}, bf16[2,3,8,32,256]{4,3,2,1,0:T(8,128)(2,1)S(1)}) custom-call(s32[7]{0:T(128)S(1)} %copy-done.10, bf16[2048,1024]{1,0:T(8,128)(2,1)S(1)} %copy-done.1, bf16[2048,1024]{1,0:T(8,128)(2,1)} %collective-permute-done.other_ref, bf16[3,8,32,256]{3,2,1,0:T(8,128)(2,1)S(1)} %get-tuple-element.17.near_ref, ...), custom_call_target="tpu_custom_call" | custom-call | tf_op jit(solution)/shard_map/stage/pallas_call | solution.py:334
  82.6 1.0 copy-done.8
  83.5 4.0 %first.1 = (s16[272,768]{1,0:T(8,128)(2,1)S(1)}, s16[272,768]{1,0:T(8,128)(2,1)S(1)}, s16[272,768]{1,0:T(8,128)(2,1)S(1)}, bf16[3,8,8,32,256]{4,3,2,1,0:T(8,128)(2,1)S(1)}) custom-call(s32[6,64]{1,0:T(8,128)S(1)} %select_reduce_fusion.place, s32[7]{0:T(128)S(1)} %copy-done.10, bf16[2,2048,1024]{2,1,0:T(8,128)(2,1)S(1)} %get-tuple-element.18.a_ref, ...), custom_call_target="tpu_custom_call" | custom-call | tf_op jit(solution)/shard_map/first/pallas_call | solution.py:360
  87.5 6.4 %second.1 = (s16[272,768]{1,0:T(8,128)(2,1)S(1)}, s16[272,768]{1,0:T(8,128)(2,1)S(1)}, s16[272,768]{1,0:T(8,128)(2,1)}, s16[272,768]{1,0:T(8,128)(2,1)S(1)}, s16[272,768]{1,0:T(8,128)(2,1)}) custom-call(s32[6,64]{1,0:T(8,128)S(1)} %select_reduce_fusion.place, s32[7]{0:T(128)S(1)} %copy-done.10, bf16[2,2048,1024]{2,1,0:T(8,128)(2,1)S(1)} %get-tuple-element.18.a_ref, ...), custom_call_target="tpu_custom_call" | custom-call | tf_op jit(solution)/shard_map/second/pallas_call | solution.py:373
  94.0 6.2 %diagonal.1 = s16[2,256,512]{2,1,0:T(8,128)(2,1)} custom-call(s32[6,64]{1,0:T(8,128)S(1)} %select_reduce_fusion.place, s32[7]{0:T(128)S(1)} %copy-done.10, s16[272,768]{1,0:T(8,128)(2,1)S(1)} %get-tuple-element.21.refs_0_, s16[272,768]{1,0:T(8,128)(2,1)S(1)} %get-tuple-element.27.refs_1_, s16[272,768]{1,0:T(8,128)(2,1)} %get-tuple-element.26.refs_2_, ...), custom_call_target="tpu_custom_call" | custom-call | tf_op jit(solution)/shard_map/diagonal/pallas_call | solution.py:392
  100.1 9.7 %all-to-all-start.2 = ((s16[64,8,512]{2,1,0:T(8,128)(2,1)}), s16[64,8,512]{2,1,0:T(8,128)(2,1)S(1)}, u32[]{:S(2)}, u32[]{:S(2)}) async-start(s16[64,8,512]{2,1,0:T(8,128)(2,1)} %bitcast.9), calls=%async_computation.2 | async-start | bytes 1048576 | tf_op jit(solution)/shard_map/all_to_all | solution.py:429
  109.8 2.8 %collective-permute-start.11 = (s16[272,768]{1,0:T(8,128)(2,1)}, s16[272,768]{1,0:T(8,128)(2,1)}, u32[]{:S(2)}, u32[]{:S(2)}) collective-permute-start(s16[272,768]{1,0:T(8,128)(2,1)} %get-tuple-element.25.refs_4_), channel_id=1, source_target_pairs={{0,8},{2,10},{4,12},{6,14},{8,0},{10,2},{12,4},{14,6},{1,9},{3,11}... | collective-permute-start | bytes 1253384 | tf_op jit(solution)/shard_map/ppermute | solution.py:410
  112.6 1.8 collective-permute-start.12
  114.4 4.2 %all-to-all-done.2.q_ref = s16[64,8,512]{2,1,0:T(8,128)(2,1)S(1)} async-done(((s16[64,8,512]{2,1,0:T(8,128)(2,1)}), s16[64,8,512]{2,1,0:T(8,128)(2,1)S(1)}, u32[]{:S(2)}, u32[]{:S(2)}) %all-to-all-start.2) | async-done | bytes 524320 | tf_op jit(solution)/shard_map/all_to_all | solution.py:429
  119.0 1.0 copy-done.2
  120.0 17.0 %all-to-all-start.3 = ((s16[128,8,512]{2,1,0:T(8,128)(2,1)}), s16[128,8,512]{2,1,0:T(8,128)(2,1)S(1)}, u32[]{:S(2)}, u32[]{:S(2)}) async-start(s16[128,8,512]{2,1,0:T(8,128)(2,1)} %copy-done.2), calls=%async_computation.3 | async-start | bytes 2097152 | tf_op jit(solution)/shard_map/all_to_all | solution.py:446
  136.9 1.3 collective-permute-start.13
  138.5 4.3 %collective-permute-start.10 = (s16[272,768]{1,0:T(8,128)(2,1)}, s16[272,768]{1,0:T(8,128)(2,1)S(1)}, u32[]{:S(2)}, u32[]{:S(2)}) collective-permute-start(s16[272,768]{1,0:T(8,128)(2,1)} %copy-done.4), channel_id=1, source_target_pairs={{0,14},{2,8},{4,10},{6,12},{8,6},{10,0},{12,2},{14,4},{1,15},{3,9}... | collective-permute-start | bytes 1253384 | tf_op jit(solution)/shard_map/ppermute | solution.py:410
  142.8 0.5 collective-permute-start.8
  143.3 4.5 %collective-permute-start.9 = (s16[272,768]{1,0:T(8,128)(2,1)S(1)}, s16[272,768]{1,0:T(8,128)(2,1)S(1)}, u32[]{:S(2)}, u32[]{:S(2)}) collective-permute-start(s16[272,768]{1,0:T(8,128)(2,1)S(1)} %get-tuple-element.23.refs_5_), channel_id=1, source_target_pairs={{0,10},{2,12},{4,14},{6,8},{8,2},{10,4},{12,6},{14,0},{1,11},{3,13... | collective-permute-start | bytes 1253384 | tf_op jit(solution)/shard_map/ppermute | solution.py:410
  147.8 9.8 %collective-permute-done.13.refs_6_ = s16[272,768]{1,0:T(8,128)(2,1)S(1)} collective-permute-done((s16[272,768]{1,0:T(8,128)(2,1)}, s16[272,768]{1,0:T(8,128)(2,1)S(1)}, u32[]{:S(2)}, u32[]{:S(2)}) %collective-permute-start.13) | collective-permute-done | bytes 417824 | tf_op jit(solution)/shard_map/ppermute | solution.py:410
  157.6 0.9 collective-permute-done.14.refs_7_
  158.5 17.5 %collective-permute-done.10.refs_3_ = s16[272,768]{1,0:T(8,128)(2,1)S(1)} collective-permute-done((s16[272,768]{1,0:T(8,128)(2,1)}, s16[272,768]{1,0:T(8,128)(2,1)S(1)}, u32[]{:S(2)}, u32[]{:S(2)}) %collective-permute-start.10) | collective-permute-done | bytes 417824 | tf_op jit(solution)/shard_map/ppermute | solution.py:410
  176.0 20.1 %collective-permute-done.8.refs_1_ = s16[272,768]{1,0:T(8,128)(2,1)S(1)} collective-permute-done((s16[272,768]{1,0:T(8,128)(2,1)}, s16[272,768]{1,0:T(8,128)(2,1)S(1)}, u32[]{:S(2)}, u32[]{:S(2)}) %collective-permute-start.8) | collective-permute-done | bytes 417824 | tf_op jit(solution)/shard_map/ppermute | solution.py:410
  196.1 2.0 %finish.1 = (bf16[128,768]{1,0:T(8,128)(2,1)S(1)}, bf16[128,768]{1,0:T(8,128)(2,1)S(1)}) custom-call(s32[6,64]{1,0:T(8,128)S(1)} %select_reduce_fusion.place, s32[7]{0:T(128)S(1)} %copy-done.10, s16[272,768]{1,0:T(8,128)(2,1)S(1)} %get-tuple-element.21.refs_0_, s16[272,768]{1,0:T(8,128)(2,1)S(1)} %collective-permute-done.8.refs_1_, ...), custom_call_target="tpu_custom_call" | custom-call | tf_op jit(solution)/shard_map/finish/pallas_call | solution.py:412
  198.2 0.9 collective-permute-start.15
  199.1 1.1 collective-permute-done.15
  200.2 0.8 maximum_select_fusion
  201.0 1.4 total.1
  (47 shorter events, 1.1 us)
Async XLA Ops:
  0.6 113.8 %copy-start = (f32[6,256,256]{2,1,0:T(8,128)S(1)}, f32[6,256,256]{2,1,0:T(8,128)}, u32[]{:S(2)}) copy-start(f32[6,256,256]{2,1,0:T(8,128)} %param.9) | copy-start | bytes 4718596
  0.6 76.6 %collective-permute-start = (bf16[2048,1024]{1,0:T(8,128)(2,1)}, bf16[2048,1024]{1,0:T(8,128)(2,1)}, u32[]{:S(2)}, u32[]{:S(2)}) collective-permute-start(bf16[2048,1024]{1,0:T(8,128)(2,1)} %own_ref.1), channel_id=1, source_target_pairs={{0,1},{1,0},{2,3},{3,2},{4,5},{5,4},{6,7},{7,6},{8,9},{9,8},{10,11... | collective-permute-start | bytes 12582920 | tf_op jit(solution)/shard_map/ppermute | solution.py:295
  4.9 8.0 %copy-start.11 = (s32[6,32]{1,0:T(8,128)S(1)}, s32[6,32]{1,0:T(8,128)}, u32[]{:S(2)}) copy-start(s32[6,32]{1,0:T(8,128)} %param.8) | copy-start | bytes 2308
  4.9 8.0 %copy-start.12 = (s32[6,32]{1,0:T(8,128)S(1)}, s32[6,32]{1,0:T(8,128)}, u32[]{:S(2)}) copy-start(s32[6,32]{1,0:T(8,128)} %param.7) | copy-start | bytes 2308
  4.9 29.0 %copy-start.10 = (s32[7]{0:T(128)S(1)}, s32[7]{0:T(128)}, u32[]{:S(2)}) copy-start(s32[7]{0:T(128)} %stack.31.where) | copy-start | bytes 88
  4.9 29.0 %all-to-all-start = ((bf16[16,2,3,32,256]{4,3,2,1,0:T(8,128)(2,1)}), bf16[16,2,3,32,256]{4,3,2,1,0:T(8,128)(2,1)S(1)}, u32[]{:S(2)}, u32[]{:S(2)}) async-start(bf16[16,2,3,32,256]{4,3,2,1,0:T(8,128)(2,1)} %share.1), calls=%async_computation | async-start | bytes 3145728 | tf_op jit(solution)/shard_map/all_to_all | solution.py:313
  34.7 0.7 copy-start.9
  35.5 16.0 %collective-permute-start.1 = (bf16[3,8,32,256]{3,2,1,0:T(8,128)(2,1)S(1)}, bf16[3,8,32,256]{3,2,1,0:T(8,128)(2,1)S(1)}, u32[]{:S(2)}, u32[]{:S(2)}) collective-permute-start(bf16[3,8,32,256]{3,2,1,0:T(8,128)(2,1)S(1)} %get-tuple-element.17.near_ref), channel_id=1, source_target_pairs={{0,32},{32,64},{64,96},{96,0},{1,33},{33,65},{65,97},{97,1},{2,34}... | collective-permute-start | bytes 1179656 | tf_op jit(solution)/shard_map/ppermute | solution.py:269
  35.7 13.6 %all-to-all-start.1 = ((bf16[8,3,32,256]{3,2,1,0:T(8,128)(2,1)}), bf16[8,3,32,256]{3,2,1,0:T(8,128)(2,1)S(1)}, u32[]{:S(2)}, u32[]{:S(2)}) async-start(bf16[8,3,32,256]{3,2,1,0:T(8,128)(2,1)} %copy-done.9), calls=%async_computation.1 | async-start | bytes 786432 | tf_op jit(solution)/shard_map/all_to_all | solution.py:328
  41.1 14.8 %collective-permute-start.4 = (bf16[3,8,32,256]{3,2,1,0:T(8,128)(2,1)S(1)}, bf16[3,8,32,256]{3,2,1,0:T(8,128)(2,1)S(1)}, u32[]{:S(2)}, u32[]{:S(2)}) collective-permute-start(bf16[3,8,32,256]{3,2,1,0:T(8,128)(2,1)S(1)} %get-tuple-element.17.near_ref), channel_id=1, source_target_pairs={{0,16},{16,0},{1,17},{17,1},{2,18},{18,2},{3,19},{19,3},{4,20},{20... | collective-permute-start | bytes 1179656 | tf_op jit(solution)/shard_map/ppermute | solution.py:325
  42.3 13.6 %collective-permute-start.2 = (bf16[3,8,32,256]{3,2,1,0:T(8,128)(2,1)S(1)}, bf16[3,8,32,256]{3,2,1,0:T(8,128)(2,1)}, u32[]{:S(2)}, u32[]{:S(2)}) collective-permute-start(bf16[3,8,32,256]{3,2,1,0:T(8,128)(2,1)S(1)} %get-tuple-element.17.near_ref), channel_id=1, source_target_pairs={{0,96},{32,0},{64,32},{96,64},{1,97},{33,1},{65,33},{97,65},{2,98}... | collective-permute-start | bytes 1179656 | tf_op jit(solution)/shard_map/ppermute | solution.py:270
  49.3 15.7 %collective-permute-start.19 = (bf16[8,3,32,256]{3,2,1,0:T(8,128)(2,1)S(1)}, bf16[8,3,32,256]{3,2,1,0:T(8,128)(2,1)S(1)}, u32[]{:S(2)}, u32[]{:S(2)}) collective-permute-start(bf16[8,3,32,256]{3,2,1,0:T(8,128)(2,1)S(1)} %all-to-all-done.1.refs_8_), channel_id=1, source_target_pairs={{0,8},{8,0},{1,9},{9,1},{2,10},{10,2},{3,11},{11,3},{4,12},{12,4},... | collective-permute-start | bytes 1179656 | tf_op jit(solution)/shard_map/ppermute | solution.py:329
  51.4 14.2 %collective-permute-start.16 = (bf16[8,3,32,256]{3,2,1,0:T(8,128)(2,1)S(1)}, bf16[8,3,32,256]{3,2,1,0:T(8,128)(2,1)S(1)}, u32[]{:S(2)}, u32[]{:S(2)}) collective-permute-start(bf16[8,3,32,256]{3,2,1,0:T(8,128)(2,1)S(1)} %all-to-all-done.1.refs_8_), channel_id=1, source_target_pairs={{0,2},{2,4},{4,6},{6,0},{1,3},{3,5},{5,7},{7,1},{8,10},{10,12},{12... | collective-permute-start | bytes 1179656 | tf_op jit(solution)/shard_map/ppermute | solution.py:269
  55.8 26.7 %copy-start.7 = (bf16[3,8,32,256]{3,2,1,0:T(8,128)(2,1)}, bf16[3,8,32,256]{3,2,1,0:T(8,128)(2,1)S(1)}, u32[]{:S(2)}) copy-start(bf16[3,8,32,256]{3,2,1,0:T(8,128)(2,1)S(1)} %collective-permute-done.4.refs_2_) | copy-start | bytes 1179652
  55.8 10.3 %collective-permute-start.6 = (bf16[3,8,32,256]{3,2,1,0:T(8,128)(2,1)S(1)}, bf16[3,8,32,256]{3,2,1,0:T(8,128)(2,1)S(1)}, u32[]{:S(2)}, u32[]{:S(2)}) collective-permute-start(bf16[3,8,32,256]{3,2,1,0:T(8,128)(2,1)S(1)} %collective-permute-done.4.refs_2_), channel_id=1, source_target_pairs={{0,96},{32,0},{64,32},{96,64},{1,97},{33,1},{65,33},{97,65},{2,98}... | collective-permute-start | bytes 1179656 | tf_op jit(solution)/shard_map/ppermute | solution.py:270
  55.8 11.7 %collective-permute-start.5 = (bf16[3,8,32,256]{3,2,1,0:T(8,128)(2,1)S(1)}, bf16[3,8,32,256]{3,2,1,0:T(8,128)(2,1)S(1)}, u32[]{:S(2)}, u32[]{:S(2)}) collective-permute-start(bf16[3,8,32,256]{3,2,1,0:T(8,128)(2,1)S(1)} %collective-permute-done.4.refs_2_), channel_id=1, source_target_pairs={{0,32},{32,64},{64,96},{96,0},{1,33},{33,65},{65,97},{97,1},{2,34}... | collective-permute-start | bytes 1179656 | tf_op jit(solution)/shard_map/ppermute | solution.py:269
  65.0 9.6 %collective-permute-start.3 = (bf16[3,8,32,256]{3,2,1,0:T(8,128)(2,1)S(1)}, bf16[3,8,32,256]{3,2,1,0:T(8,128)(2,1)S(1)}, u32[]{:S(2)}, u32[]{:S(2)}) collective-permute-start(bf16[3,8,32,256]{3,2,1,0:T(8,128)(2,1)S(1)} %collective-permute-done.1.below_ref), channel_id=1, source_target_pairs={{0,32},{32,64},{64,96},{96,0},{1,33},{33,65},{65,97},{97,1},{2,34}... | collective-permute-start | bytes 1179656 | tf_op jit(solution)/shard_map/ppermute | solution.py:271
  65.7 9.9 %collective-permute-start.21 = (bf16[8,3,32,256]{3,2,1,0:T(8,128)(2,1)S(1)}, bf16[8,3,32,256]{3,2,1,0:T(8,128)(2,1)S(1)}, u32[]{:S(2)}, u32[]{:S(2)}) collective-permute-start(bf16[8,3,32,256]{3,2,1,0:T(8,128)(2,1)S(1)} %collective-permute-done.19.refs_12_), channel_id=1, source_target_pairs={{0,6},{2,0},{4,2},{6,4},{1,7},{3,1},{5,3},{7,5},{8,14},{10,8},{12,... | collective-permute-start | bytes 1179656 | tf_op jit(solution)/shard_map/ppermute | solution.py:270
  66.2 16.4 %collective-permute-start.7 = (bf16[3,8,32,256]{3,2,1,0:T(8,128)(2,1)S(1)}, bf16[3,8,32,256]{3,2,1,0:T(8,128)(2,1)S(1)}, u32[]{:S(2)}, u32[]{:S(2)}) collective-permute-start(bf16[3,8,32,256]{3,2,1,0:T(8,128)(2,1)S(1)} %collective-permute-done.6.refs_4_), channel_id=1, source_target_pairs={{0,96},{32,0},{64,32},{96,64},{1,97},{33,1},{65,33},{97,65},{2,98}... | collective-permute-start | bytes 1179656 | tf_op jit(solution)/shard_map/ppermute | solution.py:271
  67.5 26.4 %collective-permute-start.17 = (bf16[8,3,32,256]{3,2,1,0:T(8,128)(2,1)S(1)}, bf16[8,3,32,256]{3,2,1,0:T(8,128)(2,1)S(1)}, u32[]{:S(2)}, u32[]{:S(2)}) collective-permute-start(bf16[8,3,32,256]{3,2,1,0:T(8,128)(2,1)S(1)} %all-to-all-done.1.refs_8_), channel_id=1, source_target_pairs={{0,6},{2,0},{4,2},{6,4},{1,7},{3,1},{5,3},{7,5},{8,14},{10,8},{12,... | collective-permute-start | bytes 1179656 | tf_op jit(solution)/shard_map/ppermute | solution.py:270
  74.6 19.3 %collective-permute-start.20 = (bf16[8,3,32,256]{3,2,1,0:T(8,128)(2,1)S(1)}, bf16[8,3,32,256]{3,2,1,0:T(8,128)(2,1)S(1)}, u32[]{:S(2)}, u32[]{:S(2)}) collective-permute-start(bf16[8,3,32,256]{3,2,1,0:T(8,128)(2,1)S(1)} %collective-permute-done.19.refs_12_), channel_id=1, source_target_pairs={{0,2},{2,4},{4,6},{6,0},{1,3},{3,5},{5,7},{7,1},{8,10},{10,12},{12... | collective-permute-start | bytes 1179656 | tf_op jit(solution)/shard_map/ppermute | solution.py:269
  75.5 18.4 %collective-permute-start.18 = (bf16[8,3,32,256]{3,2,1,0:T(8,128)(2,1)S(1)}, bf16[8,3,32,256]{3,2,1,0:T(8,128)(2,1)S(1)}, u32[]{:S(2)}, u32[]{:S(2)}) collective-permute-start(bf16[8,3,32,256]{3,2,1,0:T(8,128)(2,1)S(1)} %collective-permute-done.16.refs_9_), channel_id=1, source_target_pairs={{0,2},{2,4},{4,6},{6,0},{1,3},{3,5},{5,7},{7,1},{8,10},{10,12},{12... | collective-permute-start | bytes 1179656 | tf_op jit(solution)/shard_map/ppermute | solution.py:271
  77.3 16.7 %collective-permute-start.22 = (bf16[8,3,32,256]{3,2,1,0:T(8,128)(2,1)S(1)}, bf16[8,3,32,256]{3,2,1,0:T(8,128)(2,1)S(1)}, u32[]{:S(2)}, u32[]{:S(2)}) collective-permute-start(bf16[8,3,32,256]{3,2,1,0:T(8,128)(2,1)S(1)} %collective-permute-done.21.refs_14_), channel_id=1, source_target_pairs={{0,6},{2,0},{4,2},{6,4},{1,7},{3,1},{5,3},{7,5},{8,14},{10,8},{12,... | collective-permute-start | bytes 1179656 | tf_op jit(solution)/shard_map/ppermute | solution.py:271
  77.3 2.2 %copy-start.1 = (bf16[2048,1024]{1,0:T(8,128)(2,1)S(1)}, bf16[2048,1024]{1,0:T(8,128)(2,1)}, u32[]{:S(2)}) copy-start(bf16[2048,1024]{1,0:T(8,128)(2,1)} %own_ref.1) | copy-start | bytes 12582916
  82.5 1.0 copy-start.8
  87.5 6.4 %copy-start.3 = (s16[272,768]{1,0:T(8,128)(2,1)}, s16[272,768]{1,0:T(8,128)(2,1)S(1)}, u32[]{:S(2)}) copy-start(s16[272,768]{1,0:T(8,128)(2,1)S(1)} %get-tuple-element.22.refs_6_) | copy-start | bytes 1253380
  87.5 6.4 %copy-start.4 = (s16[272,768]{1,0:T(8,128)(2,1)}, s16[272,768]{1,0:T(8,128)(2,1)S(1)}, u32[]{:S(2)}) copy-start(s16[272,768]{1,0:T(8,128)(2,1)S(1)} %get-tuple-element.24.refs_7_) | copy-start | bytes 1253380
  93.9 6.2 %copy-start.5 = (s16[272,768]{1,0:T(8,128)(2,1)}, s16[272,768]{1,0:T(8,128)(2,1)S(1)}, u32[]{:S(2)}) copy-start(s16[272,768]{1,0:T(8,128)(2,1)S(1)} %get-tuple-element.28.refs_3_) | copy-start | bytes 1253380
  93.9 6.2 %copy-start.6 = (s16[272,768]{1,0:T(8,128)(2,1)}, s16[272,768]{1,0:T(8,128)(2,1)S(1)}, u32[]{:S(2)}) copy-start(s16[272,768]{1,0:T(8,128)(2,1)S(1)} %get-tuple-element.27.refs_1_) | copy-start | bytes 1253380
  100.1 18.5 %all-to-all-start.2 = ((s16[64,8,512]{2,1,0:T(8,128)(2,1)}), s16[64,8,512]{2,1,0:T(8,128)(2,1)S(1)}, u32[]{:S(2)}, u32[]{:S(2)}) async-start(s16[64,8,512]{2,1,0:T(8,128)(2,1)} %bitcast.9), calls=%async_computation.2 | async-start | bytes 1048576 | tf_op jit(solution)/shard_map/all_to_all | solution.py:429
  109.8 33.0 %collective-permute-start.11 = (s16[272,768]{1,0:T(8,128)(2,1)}, s16[272,768]{1,0:T(8,128)(2,1)}, u32[]{:S(2)}, u32[]{:S(2)}) collective-permute-start(s16[272,768]{1,0:T(8,128)(2,1)} %get-tuple-element.25.refs_4_), channel_id=1, source_target_pairs={{0,8},{2,10},{4,12},{6,14},{8,0},{10,2},{12,4},{14,6},{1,9},{3,11}... | collective-permute-start | bytes 1253384 | tf_op jit(solution)/shard_map/ppermute | solution.py:410
  112.6 30.7 %collective-permute-start.12 = (s16[272,768]{1,0:T(8,128)(2,1)}, s16[272,768]{1,0:T(8,128)(2,1)}, u32[]{:S(2)}, u32[]{:S(2)}) collective-permute-start(s16[272,768]{1,0:T(8,128)(2,1)} %get-tuple-element.26.refs_2_), channel_id=1, source_target_pairs={{0,4},{2,6},{4,0},{6,2},{8,12},{10,14},{12,8},{14,10},{1,5},{3,7},... | collective-permute-start | bytes 1253384 | tf_op jit(solution)/shard_map/ppermute | solution.py:410
  119.0 1.0 copy-start.2
  120.0 81.0 %all-to-all-start.3 = ((s16[128,8,512]{2,1,0:T(8,128)(2,1)}), s16[128,8,512]{2,1,0:T(8,128)(2,1)S(1)}, u32[]{:S(2)}, u32[]{:S(2)}) async-start(s16[128,8,512]{2,1,0:T(8,128)(2,1)} %copy-done.2), calls=%async_computation.3 | async-start | bytes 2097152 | tf_op jit(solution)/shard_map/all_to_all | solution.py:446
  136.9 20.6 %collective-permute-start.13 = (s16[272,768]{1,0:T(8,128)(2,1)}, s16[272,768]{1,0:T(8,128)(2,1)S(1)}, u32[]{:S(2)}, u32[]{:S(2)}) collective-permute-start(s16[272,768]{1,0:T(8,128)(2,1)} %copy-done.6), channel_id=1, source_target_pairs={{0,2},{2,4},{4,6},{6,0},{8,10},{10,12},{12,14},{14,8},{1,3},{3,5},... | collective-permute-start | bytes 1253384 | tf_op jit(solution)/shard_map/ppermute | solution.py:410
  138.2 20.3 %collective-permute-start.14 = (s16[272,768]{1,0:T(8,128)(2,1)}, s16[272,768]{1,0:T(8,128)(2,1)S(1)}, u32[]{:S(2)}, u32[]{:S(2)}) collective-permute-start(s16[272,768]{1,0:T(8,128)(2,1)} %copy-done.5), channel_id=1, source_target_pairs={{0,6},{2,0},{4,2},{6,4},{8,14},{10,8},{12,10},{14,12},{1,7},{3,1},... | collective-permute-start | bytes 1253384 | tf_op jit(solution)/shard_map/ppermute | solution.py:410
  138.5 37.6 %collective-permute-start.10 = (s16[272,768]{1,0:T(8,128)(2,1)}, s16[272,768]{1,0:T(8,128)(2,1)S(1)}, u32[]{:S(2)}, u32[]{:S(2)}) collective-permute-start(s16[272,768]{1,0:T(8,128)(2,1)} %copy-done.4), channel_id=1, source_target_pairs={{0,14},{2,8},{4,10},{6,12},{8,6},{10,0},{12,2},{14,4},{1,15},{3,9}... | collective-permute-start | bytes 1253384 | tf_op jit(solution)/shard_map/ppermute | solution.py:410
  142.8 53.3 %collective-permute-start.8 = (s16[272,768]{1,0:T(8,128)(2,1)}, s16[272,768]{1,0:T(8,128)(2,1)S(1)}, u32[]{:S(2)}, u32[]{:S(2)}) collective-permute-start(s16[272,768]{1,0:T(8,128)(2,1)} %copy-done.3), channel_id=1, source_target_pairs={{0,12},{2,14},{4,8},{6,10},{8,4},{10,6},{12,0},{14,2},{1,13},{3,15... | collective-permute-start | bytes 1253384 | tf_op jit(solution)/shard_map/ppermute | solution.py:410
  143.3 52.8 %collective-permute-start.9 = (s16[272,768]{1,0:T(8,128)(2,1)S(1)}, s16[272,768]{1,0:T(8,128)(2,1)S(1)}, u32[]{:S(2)}, u32[]{:S(2)}) collective-permute-start(s16[272,768]{1,0:T(8,128)(2,1)S(1)} %get-tuple-element.23.refs_5_), channel_id=1, source_target_pairs={{0,10},{2,12},{4,14},{6,8},{8,2},{10,4},{12,6},{14,0},{1,11},{3,13... | collective-permute-start | bytes 1253384 | tf_op jit(solution)/shard_map/ppermute | solution.py:410
  198.2 2.0 collective-permute-start.15
where the time goes:
time: 203 us; the launch traced here: 202 us
  waiting for transfers between devices  96.9 us (48%)
  starting transfers between devices  71 us (35%)
  Pallas kernels  27 us (13%)
  local copies, waits for them, and re-layouts  5.59 us (3%)
    ppermute x7, waiting for transfers between devices, update(): sums.append(lax.ppermute(coded[j], HY, to))  48.4 us
    all_to_all x1, waiting for transfers between devices, update(): lax.all_to_all(share, ('h', 'y', 'c'), split_axis=0, concat_axis=0, tiled...  20.8 us
    all_to_all x1, starting transfers between devices, update(): lax.all_to_all(piece, CHIPS + ('c',), split_axis=0, concat_axis=0, tiled=...  17 us
    ppermute x7, starting transfers between devices, update(): sums.append(lax.ppermute(coded[j], HY, to))  15.4 us
    all_to_all x1, starting transfers between devices, update(): diag = lax.all_to_all(diag, CHIPS, split_axis=0, concat_axis=0, tiled=True)  9.68 us
    all_to_all x1, starting transfers between devices, update(): lax.all_to_all(share, ('h', 'y', 'c'), split_axis=0, concat_axis=0, tiled...  7.98 us
    all_to_all x1, waiting for transfers between devices, update(): own = lax.all_to_all(own, XL, split_axis=0, concat_axis=0, tiled=True)  6.46 us
    ppermute x1, waiting for transfers between devices, update(): across = lax.ppermute(own, 'h', CORE_SWAP)  6.46 us
  transfers between devices with their start and end apart: 27, of which 12 were waited for; matrix products, arithmetic and copies ran while one was open for 1% of the time, Pallas kernels for 10%

commit v1 on v0

--- a/solution.py
+++ b/solution.py
@@ -21,6 +21,7 @@
 LEVELS = 32000.0
 LOWEST = -100.0
 LANES = 128
+TAIL = 8
 
 
 def level_of(top):
@@ -158,7 +159,7 @@
                 left = a_ref[lax.div(s, half), :, pl.ds(start, size)]
                 values += jnp.dot(left, panel[k, s].reshape(size, size), preferred_element_type=F32)
             level = level_of(jnp.max(jnp.abs(values), axis=0, keepdims=True))
-            tail = jnp.broadcast_to(level, (16, size)).astype(jnp.int32).astype(I16)
+            tail = jnp.broadcast_to(level, (TAIL, size)).astype(jnp.int32).astype(I16)
             store(jnp.concatenate([code(values, level), tail], axis=0))
 
         @pl.when(jnp.logical_and(wanted, few))
@@ -171,7 +172,7 @@
 
         @pl.when(jnp.logical_not(wanted))
         def _():
-            store(jnp.zeros((size + 16, size), I16))
+            store(jnp.zeros((size + TAIL, size), I16))
 
 
 def diagonal_kernel(place, where, *refs):
@@ -189,17 +190,15 @@
 
                 @pl.when(place[core * members + k, group * count + tile] >= 0)
                 def _():
-                    own = ref[:, k].reshape(size, size)
+                    own = jnp.transpose(ref[:, k].reshape(size, size))
                     rest = plain(q_ref[:size, cols])
                     high = rest.astype(BF16)
                     low = (rest - high.astype(F32)).astype(BF16)
-                    total = sum(
-                        lax.dot_general(
-                            own, term, (((0,), (0,)), ((), ())), preferred_element_type=F32
-                        )
-                        for term in (high, low)
+                    both = jnp.dot(
+                        own, jnp.concatenate([high, low], axis=1), preferred_element_type=F32
                     )
-                    block[:, cols] -= total * scale_of(plain(q_ref[size : size + 16, cols])[:1])
+                    total = both[:, :size] + both[:, size:]
+                    block[:, cols] -= total * scale_of(plain(q_ref[size : size + TAIL, cols])[:1])
 
     values = block[...]
     level = level_of(jnp.max(jnp.abs(values), keepdims=True))
@@ -221,7 +220,7 @@
         cols = slice(k * size, (k + 1) * size)
         total = jnp.zeros((size, size), F32)
         for ref in parts:
-            scale = scale_of(plain(ref[size : size + 16, cols])[:1])
+            scale = scale_of(plain(ref[size : size + TAIL, cols])[:1])
             total += plain(ref[:size, cols]) * scale
         keep = place[core * members + k, mine] >= 0
         rounded = jnp.where(keep, -total, jnp.zeros_like(total)).astype(BF16)
@@ -353,7 +352,7 @@
         return pl.BlockSpec((NC, size, cols), index)
 
     panel = jax.ShapeDtypeStruct((members, window, groups, part, size), BF16)
-    block = jax.ShapeDtypeStruct((size + 16, width), I16)
+    block = jax.ShapeDtypeStruct((size + TAIL, width), I16)
     order = pltpu.SMEM((members, window + 1), jnp.int32)
     params = pltpu.CompilerParams(vmem_limit_bytes=20 << 20)
     late, early = tuple(range(5)), tuple(range(5, chips))
@@ -400,7 +399,7 @@
     )(place, where, *coded, *row_parts)
 
     sums = [coded[0]]
-    for shifts in ((6, 5, 7), (4, 2), (1, 3)):
+    for shifts in ((6, 5), (7, 2, 4, 1, 3)):
         for j in shifts:
             to = [
                 (h * NY + y, (h + j // NY) % NH * NY + (y + j) % NY)

time: 203 us -> 203 us (level)
  no operation moved by 1% of the time
where the time goes in v1:
time: 203 us; the launch traced here: 202 us
  waiting for transfers between devices  95.6 us (47%)
  starting transfers between devices  70.8 us (35%)
  Pallas kernels  27.6 us (14%)
  local copies, waits for them, and re-layouts  5.27 us (3%)
    ppermute x7, waiting for transfers between devices, update(): sums.append(lax.ppermute(coded[j], HY, to))  46.9 us
    all_to_all x1, waiting for transfers between devices, update(): lax.all_to_all(share, ('h', 'y', 'c'), split_axis=0, concat_axis=0, tiled...  20.8 us
    all_to_all x1, starting transfers between devices, update(): lax.all_to_all(piece, CHIPS + ('c',), split_axis=0, concat_axis=0, tiled=...  16.7 us
    ppermute x7, starting transfers between devices, update(): sums.append(lax.ppermute(coded[j], HY, to))  15.4 us
    all_to_all x1, starting transfers between devices, update(): diag = lax.all_to_all(diag, CHIPS, split_axis=0, concat_axis=0, tiled=True)  9.74 us
    all_to_all x1, starting transfers between devices, update(): lax.all_to_all(share, ('h', 'y', 'c'), split_axis=0, concat_axis=0, tiled...  7.98 us
    all_to_all x1, waiting for transfers between devices, update(): own = lax.all_to_all(own, XL, split_axis=0, concat_axis=0, tiled=True)  6.46 us
    ppermute x1, waiting for transfers between devices, update(): across = lax.ppermute(own, 'h', CORE_SWAP)  6.46 us
  transfers between devices with their start and end apart: 27, of which 12 were waited for; matrix products, arithmetic and copies ran while one was open for 1% of the time, Pallas kernels for 10%

profile of v1, /device:TPU:15, one launch (start us, length us, event | category | flops | bytes accessed | tf_op | source)
XLA Modules:
  0.0 202.1 jit_solution(4252191211670476020)
XLA Ops:
  0.6 0.8 collective-permute-start
  1.4 0.7 stack.31.where
  2.1 2.8 %share.1 = bf16[16,2,3,32,256]{4,3,2,1,0:T(8,128)(2,1)} custom-call(s32[7]{0:T(128)} %stack.31.where, bf16[2,6,256,256]{3,2,1,0:T(8,128)(2,1)} %bitcast.18), custom_call_target="tpu_custom_call" | custom-call | tf_op jit(solution)/shard_map/share/pallas_call | solution.py:301
  4.9 8.0 %all-to-all-start = ((bf16[16,2,3,32,256]{4,3,2,1,0:T(8,128)(2,1)}), bf16[16,2,3,32,256]{4,3,2,1,0:T(8,128)(2,1)S(1)}, u32[]{:S(2)}, u32[]{:S(2)}) async-start(bf16[16,2,3,32,256]{4,3,2,1,0:T(8,128)(2,1)} %share.1), calls=%async_computation | async-start | bytes 3145728 | tf_op jit(solution)/shard_map/all_to_all | solution.py:312
  13.1 20.8 %all-to-all-done = bf16[16,2,3,32,256]{4,3,2,1,0:T(8,128)(2,1)S(1)} async-done(((bf16[16,2,3,32,256]{4,3,2,1,0:T(8,128)(2,1)}), bf16[16,2,3,32,256]{4,3,2,1,0:T(8,128)(2,1)S(1)}, u32[]{:S(2)}, u32[]{:S(2)}) %all-to-all-start) | async-done | bytes 1572896 | tf_op jit(solution)/shard_map/all_to_all | solution.py:312
  33.9 0.8 pick.1
  34.7 0.7 copy-done.8
  35.7 5.4 %all-to-all-start.1 = ((bf16[8,3,32,256]{3,2,1,0:T(8,128)(2,1)}), bf16[8,3,32,256]{3,2,1,0:T(8,128)(2,1)S(1)}, u32[]{:S(2)}, u32[]{:S(2)}) async-start(bf16[8,3,32,256]{3,2,1,0:T(8,128)(2,1)} %copy-done.8), calls=%async_computation.1 | async-start | bytes 786432 | tf_op jit(solution)/shard_map/all_to_all | solution.py:327
  41.1 1.2 collective-permute-start.4
  42.3 0.6 collective-permute-start.2
  42.8 6.5 %all-to-all-done.1.refs_8_ = bf16[8,3,32,256]{3,2,1,0:T(8,128)(2,1)S(1)} async-done(((bf16[8,3,32,256]{3,2,1,0:T(8,128)(2,1)}), bf16[8,3,32,256]{3,2,1,0:T(8,128)(2,1)S(1)}, u32[]{:S(2)}, u32[]{:S(2)}) %all-to-all-start.1) | async-done | bytes 393248 | tf_op jit(solution)/shard_map/all_to_all | solution.py:327
  49.3 2.1 %collective-permute-start.19 = (bf16[8,3,32,256]{3,2,1,0:T(8,128)(2,1)S(1)}, bf16[8,3,32,256]{3,2,1,0:T(8,128)(2,1)S(1)}, u32[]{:S(2)}, u32[]{:S(2)}) collective-permute-start(bf16[8,3,32,256]{3,2,1,0:T(8,128)(2,1)S(1)} %all-to-all-done.1.refs_8_), channel_id=1, source_target_pairs={{0,8},{8,0},{1,9},{9,1},{2,10},{10,2},{3,11},{11,3},{4,12},{12,4},... | collective-permute-start | bytes 1179656 | tf_op jit(solution)/shard_map/ppermute | solution.py:328
  51.4 1.3 collective-permute-start.16
  52.8 3.1 %collective-permute-done.4.refs_2_ = bf16[3,8,32,256]{3,2,1,0:T(8,128)(2,1)S(1)} collective-permute-done((bf16[3,8,32,256]{3,2,1,0:T(8,128)(2,1)S(1)}, bf16[3,8,32,256]{3,2,1,0:T(8,128)(2,1)S(1)}, u32[]{:S(2)}, u32[]{:S(2)}) %collective-permute-start.4) | collective-permute-done | bytes 393248 | tf_op jit(solution)/shard_map/ppermute | solution.py:324
  55.8 2.7 %collective-permute-start.5 = (bf16[3,8,32,256]{3,2,1,0:T(8,128)(2,1)S(1)}, bf16[3,8,32,256]{3,2,1,0:T(8,128)(2,1)S(1)}, u32[]{:S(2)}, u32[]{:S(2)}) collective-permute-start(bf16[3,8,32,256]{3,2,1,0:T(8,128)(2,1)S(1)} %collective-permute-done.4.refs_2_), channel_id=1, source_target_pairs={{0,32},{32,64},{64,96},{96,0},{1,33},{33,65},{65,97},{97,1},{2,34}... | collective-permute-start | bytes 1179656 | tf_op jit(solution)/shard_map/ppermute | solution.py:268
  58.5 6.5 %collective-permute-done.19.refs_12_ = bf16[8,3,32,256]{3,2,1,0:T(8,128)(2,1)S(1)} collective-permute-done((bf16[8,3,32,256]{3,2,1,0:T(8,128)(2,1)S(1)}, bf16[8,3,32,256]{3,2,1,0:T(8,128)(2,1)S(1)}, u32[]{:S(2)}, u32[]{:S(2)}) %collective-permute-start.19) | collective-permute-done | bytes 393248 | tf_op jit(solution)/shard_map/ppermute | solution.py:328
  65.0 0.7 collective-permute-start.3
  65.7 0.4 collective-permute-start.21
  66.2 1.4 collective-permute-start.7
  67.5 0.7 collective-permute-start.17
  68.2 6.4 %collective-permute-done.3.refs_1_ = bf16[3,8,32,256]{3,2,1,0:T(8,128)(2,1)S(1)} collective-permute-done((bf16[3,8,32,256]{3,2,1,0:T(8,128)(2,1)S(1)}, bf16[3,8,32,256]{3,2,1,0:T(8,128)(2,1)S(1)}, u32[]{:S(2)}, u32[]{:S(2)}) %collective-permute-start.3) | collective-permute-done | bytes 393248 | tf_op jit(solution)/shard_map/ppermute | solution.py:270
  74.6 0.9 collective-permute-start.20
  75.5 1.7 collective-permute-start.18
  77.3 2.2 %copy-done.1 = bf16[2048,1024]{1,0:T(8,128)(2,1)S(1)} copy-done((bf16[2048,1024]{1,0:T(8,128)(2,1)S(1)}, bf16[2048,1024]{1,0:T(8,128)(2,1)}, u32[]{:S(2)}) %copy-start.1) | copy-done | bytes 4194328
  79.5 3.0 %stage.1 = (bf16[2,2048,1024]{2,1,0:T(8,128)(2,1)S(1)}, bf16[2,3,8,32,256]{4,3,2,1,0:T(8,128)(2,1)S(1)}) custom-call(s32[7]{0:T(128)S(1)} %copy-done.10, bf16[2048,1024]{1,0:T(8,128)(2,1)S(1)} %copy-done.1, bf16[2048,1024]{1,0:T(8,128)(2,1)} %collective-permute-done.other_ref, bf16[3,8,32,256]{3,2,1,0:T(8,128)(2,1)S(1)} %get-tuple-element.17.near_ref, ...), custom_call_target="tpu_custom_call" | custom-call | tf_op jit(solution)/shard_map/stage/pallas_call | solution.py:333
  82.5 4.0 %first.1 = (s16[264,768]{1,0:T(8,128)(2,1)S(1)}, s16[264,768]{1,0:T(8,128)(2,1)S(1)}, s16[264,768]{1,0:T(8,128)(2,1)S(1)}, bf16[3,8,8,32,256]{4,3,2,1,0:T(8,128)(2,1)S(1)}) custom-call(s32[6,64]{1,0:T(8,128)S(1)} %select_reduce_fusion.place, s32[7]{0:T(128)S(1)} %copy-done.10, bf16[2,2048,1024]{2,1,0:T(8,128)(2,1)S(1)} %get-tuple-element.18.a_ref, ...), custom_call_target="tpu_custom_call" | custom-call | tf_op jit(solution)/shard_map/first/pallas_call | solution.py:359
  86.6 6.4 %second.1 = (s16[264,768]{1,0:T(8,128)(2,1)S(1)}, s16[264,768]{1,0:T(8,128)(2,1)S(1)}, s16[264,768]{1,0:T(8,128)(2,1)}, s16[264,768]{1,0:T(8,128)(2,1)S(1)}, s16[264,768]{1,0:T(8,128)(2,1)}) custom-call(s32[6,64]{1,0:T(8,128)S(1)} %select_reduce_fusion.place, s32[7]{0:T(128)S(1)} %copy-done.10, bf16[2,2048,1024]{2,1,0:T(8,128)(2,1)S(1)} %get-tuple-element.18.a_ref, ...), custom_call_target="tpu_custom_call" | custom-call | tf_op jit(solution)/shard_map/second/pallas_call | solution.py:372
  93.0 6.1 %diagonal.1 = s16[2,256,512]{2,1,0:T(8,128)(2,1)} custom-call(s32[6,64]{1,0:T(8,128)S(1)} %select_reduce_fusion.place, s32[7]{0:T(128)S(1)} %copy-done.10, s16[264,768]{1,0:T(8,128)(2,1)S(1)} %get-tuple-element.21.refs_0_, s16[264,768]{1,0:T(8,128)(2,1)S(1)} %get-tuple-element.27.refs_1_, s16[264,768]{1,0:T(8,128)(2,1)} %get-tuple-element.25.refs_2_, ...), custom_call_target="tpu_custom_call" | custom-call | tf_op jit(solution)/shard_map/diagonal/pallas_call | solution.py:391
  99.2 9.7 %all-to-all-start.2 = ((s16[64,8,512]{2,1,0:T(8,128)(2,1)}), s16[64,8,512]{2,1,0:T(8,128)(2,1)S(1)}, u32[]{:S(2)}, u32[]{:S(2)}) async-start(s16[64,8,512]{2,1,0:T(8,128)(2,1)} %bitcast.9), calls=%async_computation.2 | async-start | bytes 1048576 | tf_op jit(solution)/shard_map/all_to_all | solution.py:428
  108.9 1.9 collective-permute-start.11
  110.8 2.7 %collective-permute-start.12 = (s16[264,768]{1,0:T(8,128)(2,1)}, s16[264,768]{1,0:T(8,128)(2,1)}, u32[]{:S(2)}, u32[]{:S(2)}) collective-permute-start(s16[264,768]{1,0:T(8,128)(2,1)} %get-tuple-element.26.refs_4_), channel_id=1, source_target_pairs={{0,8},{2,10},{4,12},{6,14},{8,0},{10,2},{12,4},{14,6},{1,9},{3,11}... | collective-permute-start | bytes 1216520 | tf_op jit(solution)/shard_map/ppermute | solution.py:409
  113.6 4.1 %all-to-all-done.2.q_ref = s16[64,8,512]{2,1,0:T(8,128)(2,1)S(1)} async-done(((s16[64,8,512]{2,1,0:T(8,128)(2,1)}), s16[64,8,512]{2,1,0:T(8,128)(2,1)S(1)}, u32[]{:S(2)}, u32[]{:S(2)}) %all-to-all-start.2) | async-done | bytes 524320 | tf_op jit(solution)/shard_map/all_to_all | solution.py:428
  118.1 1.0 copy-done.2
  119.1 16.7 %all-to-all-start.3 = ((s16[128,8,512]{2,1,0:T(8,128)(2,1)}), s16[128,8,512]{2,1,0:T(8,128)(2,1)S(1)}, u32[]{:S(2)}, u32[]{:S(2)}) async-start(s16[128,8,512]{2,1,0:T(8,128)(2,1)} %copy-done.2), calls=%async_computation.3 | async-start | bytes 2097152 | tf_op jit(solution)/shard_map/all_to_all | solution.py:445
  135.8 1.3 collective-permute-start.13
  137.3 4.3 %collective-permute-start.10 = (s16[264,768]{1,0:T(8,128)(2,1)}, s16[264,768]{1,0:T(8,128)(2,1)S(1)}, u32[]{:S(2)}, u32[]{:S(2)}) collective-permute-start(s16[264,768]{1,0:T(8,128)(2,1)} %copy-done.5), channel_id=1, source_target_pairs={{0,14},{2,8},{4,10},{6,12},{8,6},{10,0},{12,2},{14,4},{1,15},{3,9}... | collective-permute-start | bytes 1216520 | tf_op jit(solution)/shard_map/ppermute | solution.py:409
  141.6 0.5 collective-permute-start.8
  142.1 4.5 %collective-permute-start.9 = (s16[264,768]{1,0:T(8,128)(2,1)}, s16[264,768]{1,0:T(8,128)(2,1)S(1)}, u32[]{:S(2)}, u32[]{:S(2)}) collective-permute-start(s16[264,768]{1,0:T(8,128)(2,1)} %copy-done.3), channel_id=1, source_target_pairs={{0,10},{2,12},{4,14},{6,8},{8,2},{10,4},{12,6},{14,0},{1,11},{3,13... | collective-permute-start | bytes 1216520 | tf_op jit(solution)/shard_map/ppermute | solution.py:409
  146.6 9.5 %collective-permute-done.13.refs_6_ = s16[264,768]{1,0:T(8,128)(2,1)S(1)} collective-permute-done((s16[264,768]{1,0:T(8,128)(2,1)}, s16[264,768]{1,0:T(8,128)(2,1)S(1)}, u32[]{:S(2)}, u32[]{:S(2)}) %collective-permute-start.13) | collective-permute-done | bytes 405536 | tf_op jit(solution)/shard_map/ppermute | solution.py:409
  156.1 0.9 collective-permute-done.14.refs_7_
  157.1 16.8 %collective-permute-done.10.refs_3_ = s16[264,768]{1,0:T(8,128)(2,1)S(1)} collective-permute-done((s16[264,768]{1,0:T(8,128)(2,1)}, s16[264,768]{1,0:T(8,128)(2,1)S(1)}, u32[]{:S(2)}, u32[]{:S(2)}) %collective-permute-start.10) | collective-permute-done | bytes 405536 | tf_op jit(solution)/shard_map/ppermute | solution.py:409
  173.9 19.6 %collective-permute-done.8.refs_1_ = s16[264,768]{1,0:T(8,128)(2,1)S(1)} collective-permute-done((s16[264,768]{1,0:T(8,128)(2,1)}, s16[264,768]{1,0:T(8,128)(2,1)S(1)}, u32[]{:S(2)}, u32[]{:S(2)}) %collective-permute-start.8) | collective-permute-done | bytes 405536 | tf_op jit(solution)/shard_map/ppermute | solution.py:409
  193.5 2.6 %finish.1 = (bf16[128,768]{1,0:T(8,128)(2,1)S(1)}, bf16[128,768]{1,0:T(8,128)(2,1)}) custom-call(s32[6,64]{1,0:T(8,128)S(1)} %select_reduce_fusion.place, s32[7]{0:T(128)S(1)} %copy-done.10, s16[264,768]{1,0:T(8,128)(2,1)S(1)} %get-tuple-element.21.refs_0_, s16[264,768]{1,0:T(8,128)(2,1)S(1)} %collective-permute-done.8.refs_1_, ...), custom_call_target="tpu_custom_call" | custom-call | tf_op jit(solution)/shard_map/finish/pallas_call | solution.py:411
  196.1 0.7 copy-done.9
  196.8 0.8 collective-permute-start.15
  197.6 1.3 collective-permute-done.15
  198.9 1.9 maximum_select_fusion
  200.7 1.4 total.1
  (47 shorter events, 1.2 us)
Async XLA Ops:
  0.6 112.9 %copy-start = (f32[6,256,256]{2,1,0:T(8,128)S(1)}, f32[6,256,256]{2,1,0:T(8,128)}, u32[]{:S(2)}) copy-start(f32[6,256,256]{2,1,0:T(8,128)} %param.9) | copy-start | bytes 4718596
  0.6 76.6 %collective-permute-start = (bf16[2048,1024]{1,0:T(8,128)(2,1)}, bf16[2048,1024]{1,0:T(8,128)(2,1)}, u32[]{:S(2)}, u32[]{:S(2)}) collective-permute-start(bf16[2048,1024]{1,0:T(8,128)(2,1)} %own_ref.1), channel_id=1, source_target_pairs={{0,1},{1,0},{2,3},{3,2},{4,5},{5,4},{6,7},{7,6},{8,9},{9,8},{10,11... | collective-permute-start | bytes 12582920 | tf_op jit(solution)/shard_map/ppermute | solution.py:294
  4.9 8.0 %copy-start.11 = (s32[6,32]{1,0:T(8,128)S(1)}, s32[6,32]{1,0:T(8,128)}, u32[]{:S(2)}) copy-start(s32[6,32]{1,0:T(8,128)} %param.8) | copy-start | bytes 2308
  4.9 8.0 %copy-start.12 = (s32[6,32]{1,0:T(8,128)S(1)}, s32[6,32]{1,0:T(8,128)}, u32[]{:S(2)}) copy-start(s32[6,32]{1,0:T(8,128)} %param.7) | copy-start | bytes 2308
  4.9 29.0 %copy-start.10 = (s32[7]{0:T(128)S(1)}, s32[7]{0:T(128)}, u32[]{:S(2)}) copy-start(s32[7]{0:T(128)} %stack.31.where) | copy-start | bytes 88
  4.9 29.0 %all-to-all-start = ((bf16[16,2,3,32,256]{4,3,2,1,0:T(8,128)(2,1)}), bf16[16,2,3,32,256]{4,3,2,1,0:T(8,128)(2,1)S(1)}, u32[]{:S(2)}, u32[]{:S(2)}) async-start(bf16[16,2,3,32,256]{4,3,2,1,0:T(8,128)(2,1)} %share.1), calls=%async_computation | async-start | bytes 3145728 | tf_op jit(solution)/shard_map/all_to_all | solution.py:312
  34.7 0.7 copy-start.8
  35.5 16.0 %collective-permute-start.1 = (bf16[3,8,32,256]{3,2,1,0:T(8,128)(2,1)S(1)}, bf16[3,8,32,256]{3,2,1,0:T(8,128)(2,1)S(1)}, u32[]{:S(2)}, u32[]{:S(2)}) collective-permute-start(bf16[3,8,32,256]{3,2,1,0:T(8,128)(2,1)S(1)} %get-tuple-element.17.near_ref), channel_id=1, source_target_pairs={{0,32},{32,64},{64,96},{96,0},{1,33},{33,65},{65,97},{97,1},{2,34}... | collective-permute-start | bytes 1179656 | tf_op jit(solution)/shard_map/ppermute | solution.py:268
  35.7 13.6 %all-to-all-start.1 = ((bf16[8,3,32,256]{3,2,1,0:T(8,128)(2,1)}), bf16[8,3,32,256]{3,2,1,0:T(8,128)(2,1)S(1)}, u32[]{:S(2)}, u32[]{:S(2)}) async-start(bf16[8,3,32,256]{3,2,1,0:T(8,128)(2,1)} %copy-done.8), calls=%async_computation.1 | async-start | bytes 786432 | tf_op jit(solution)/shard_map/all_to_all | solution.py:327
  41.1 14.8 %collective-permute-start.4 = (bf16[3,8,32,256]{3,2,1,0:T(8,128)(2,1)S(1)}, bf16[3,8,32,256]{3,2,1,0:T(8,128)(2,1)S(1)}, u32[]{:S(2)}, u32[]{:S(2)}) collective-permute-start(bf16[3,8,32,256]{3,2,1,0:T(8,128)(2,1)S(1)} %get-tuple-element.17.near_ref), channel_id=1, source_target_pairs={{0,16},{16,0},{1,17},{17,1},{2,18},{18,2},{3,19},{19,3},{4,20},{20... | collective-permute-start | bytes 1179656 | tf_op jit(solution)/shard_map/ppermute | solution.py:324
  42.3 13.6 %collective-permute-start.2 = (bf16[3,8,32,256]{3,2,1,0:T(8,128)(2,1)S(1)}, bf16[3,8,32,256]{3,2,1,0:T(8,128)(2,1)}, u32[]{:S(2)}, u32[]{:S(2)}) collective-permute-start(bf16[3,8,32,256]{3,2,1,0:T(8,128)(2,1)S(1)} %get-tuple-element.17.near_ref), channel_id=1, source_target_pairs={{0,96},{32,0},{64,32},{96,64},{1,97},{33,1},{65,33},{97,65},{2,98}... | collective-permute-start | bytes 1179656 | tf_op jit(solution)/shard_map/ppermute | solution.py:269
  49.3 15.7 %collective-permute-start.19 = (bf16[8,3,32,256]{3,2,1,0:T(8,128)(2,1)S(1)}, bf16[8,3,32,256]{3,2,1,0:T(8,128)(2,1)S(1)}, u32[]{:S(2)}, u32[]{:S(2)}) collective-permute-start(bf16[8,3,32,256]{3,2,1,0:T(8,128)(2,1)S(1)} %all-to-all-done.1.refs_8_), channel_id=1, source_target_pairs={{0,8},{8,0},{1,9},{9,1},{2,10},{10,2},{3,11},{11,3},{4,12},{12,4},... | collective-permute-start | bytes 1179656 | tf_op jit(solution)/shard_map/ppermute | solution.py:328
  51.4 14.2 %collective-permute-start.16 = (bf16[8,3,32,256]{3,2,1,0:T(8,128)(2,1)S(1)}, bf16[8,3,32,256]{3,2,1,0:T(8,128)(2,1)S(1)}, u32[]{:S(2)}, u32[]{:S(2)}) collective-permute-start(bf16[8,3,32,256]{3,2,1,0:T(8,128)(2,1)S(1)} %all-to-all-done.1.refs_8_), channel_id=1, source_target_pairs={{0,2},{2,4},{4,6},{6,0},{1,3},{3,5},{5,7},{7,1},{8,10},{10,12},{12... | collective-permute-start | bytes 1179656 | tf_op jit(solution)/shard_map/ppermute | solution.py:268
  55.8 10.3 %collective-permute-start.6 = (bf16[3,8,32,256]{3,2,1,0:T(8,128)(2,1)S(1)}, bf16[3,8,32,256]{3,2,1,0:T(8,128)(2,1)S(1)}, u32[]{:S(2)}, u32[]{:S(2)}) collective-permute-start(bf16[3,8,32,256]{3,2,1,0:T(8,128)(2,1)S(1)} %collective-permute-done.4.refs_2_), channel_id=1, source_target_pairs={{0,96},{32,0},{64,32},{96,64},{1,97},{33,1},{65,33},{97,65},{2,98}... | collective-permute-start | bytes 1179656 | tf_op jit(solution)/shard_map/ppermute | solution.py:269
  55.8 11.7 %collective-permute-start.5 = (bf16[3,8,32,256]{3,2,1,0:T(8,128)(2,1)S(1)}, bf16[3,8,32,256]{3,2,1,0:T(8,128)(2,1)S(1)}, u32[]{:S(2)}, u32[]{:S(2)}) collective-permute-start(bf16[3,8,32,256]{3,2,1,0:T(8,128)(2,1)S(1)} %collective-permute-done.4.refs_2_), channel_id=1, source_target_pairs={{0,32},{32,64},{64,96},{96,0},{1,33},{33,65},{65,97},{97,1},{2,34}... | collective-permute-start | bytes 1179656 | tf_op jit(solution)/shard_map/ppermute | solution.py:268
  65.0 9.6 %collective-permute-start.3 = (bf16[3,8,32,256]{3,2,1,0:T(8,128)(2,1)S(1)}, bf16[3,8,32,256]{3,2,1,0:T(8,128)(2,1)S(1)}, u32[]{:S(2)}, u32[]{:S(2)}) collective-permute-start(bf16[3,8,32,256]{3,2,1,0:T(8,128)(2,1)S(1)} %collective-permute-done.1.below_ref), channel_id=1, source_target_pairs={{0,32},{32,64},{64,96},{96,0},{1,33},{33,65},{65,97},{97,1},{2,34}... | collective-permute-start | bytes 1179656 | tf_op jit(solution)/shard_map/ppermute | solution.py:270
  65.7 9.9 %collective-permute-start.21 = (bf16[8,3,32,256]{3,2,1,0:T(8,128)(2,1)S(1)}, bf16[8,3,32,256]{3,2,1,0:T(8,128)(2,1)S(1)}, u32[]{:S(2)}, u32[]{:S(2)}) collective-permute-start(bf16[8,3,32,256]{3,2,1,0:T(8,128)(2,1)S(1)} %collective-permute-done.19.refs_12_), channel_id=1, source_target_pairs={{0,6},{2,0},{4,2},{6,4},{1,7},{3,1},{5,3},{7,5},{8,14},{10,8},{12,... | collective-permute-start | bytes 1179656 | tf_op jit(solution)/shard_map/ppermute | solution.py:269
  66.2 16.4 %collective-permute-start.7 = (bf16[3,8,32,256]{3,2,1,0:T(8,128)(2,1)S(1)}, bf16[3,8,32,256]{3,2,1,0:T(8,128)(2,1)S(1)}, u32[]{:S(2)}, u32[]{:S(2)}) collective-permute-start(bf16[3,8,32,256]{3,2,1,0:T(8,128)(2,1)S(1)} %collective-permute-done.6.refs_4_), channel_id=1, source_target_pairs={{0,96},{32,0},{64,32},{96,64},{1,97},{33,1},{65,33},{97,65},{2,98}... | collective-permute-start | bytes 1179656 | tf_op jit(solution)/shard_map/ppermute | solution.py:270
  67.5 25.4 %collective-permute-start.17 = (bf16[8,3,32,256]{3,2,1,0:T(8,128)(2,1)S(1)}, bf16[8,3,32,256]{3,2,1,0:T(8,128)(2,1)S(1)}, u32[]{:S(2)}, u32[]{:S(2)}) collective-permute-start(bf16[8,3,32,256]{3,2,1,0:T(8,128)(2,1)S(1)} %all-to-all-done.1.refs_8_), channel_id=1, source_target_pairs={{0,6},{2,0},{4,2},{6,4},{1,7},{3,1},{5,3},{7,5},{8,14},{10,8},{12,... | collective-permute-start | bytes 1179656 | tf_op jit(solution)/shard_map/ppermute | solution.py:269
  74.6 18.4 %collective-permute-start.20 = (bf16[8,3,32,256]{3,2,1,0:T(8,128)(2,1)S(1)}, bf16[8,3,32,256]{3,2,1,0:T(8,128)(2,1)S(1)}, u32[]{:S(2)}, u32[]{:S(2)}) collective-permute-start(bf16[8,3,32,256]{3,2,1,0:T(8,128)(2,1)S(1)} %collective-permute-done.19.refs_12_), channel_id=1, source_target_pairs={{0,2},{2,4},{4,6},{6,0},{1,3},{3,5},{5,7},{7,1},{8,10},{10,12},{12... | collective-permute-start | bytes 1179656 | tf_op jit(solution)/shard_map/ppermute | solution.py:268
  75.5 17.5 %collective-permute-start.18 = (bf16[8,3,32,256]{3,2,1,0:T(8,128)(2,1)S(1)}, bf16[8,3,32,256]{3,2,1,0:T(8,128)(2,1)S(1)}, u32[]{:S(2)}, u32[]{:S(2)}) collective-permute-start(bf16[8,3,32,256]{3,2,1,0:T(8,128)(2,1)S(1)} %collective-permute-done.16.refs_9_), channel_id=1, source_target_pairs={{0,2},{2,4},{4,6},{6,0},{1,3},{3,5},{5,7},{7,1},{8,10},{10,12},{12... | collective-permute-start | bytes 1179656 | tf_op jit(solution)/shard_map/ppermute | solution.py:270
  77.3 15.7 %collective-permute-start.22 = (bf16[8,3,32,256]{3,2,1,0:T(8,128)(2,1)S(1)}, bf16[8,3,32,256]{3,2,1,0:T(8,128)(2,1)S(1)}, u32[]{:S(2)}, u32[]{:S(2)}) collective-permute-start(bf16[8,3,32,256]{3,2,1,0:T(8,128)(2,1)S(1)} %collective-permute-done.21.refs_14_), channel_id=1, source_target_pairs={{0,6},{2,0},{4,2},{6,4},{1,7},{3,1},{5,3},{7,5},{8,14},{10,8},{12,... | collective-permute-start | bytes 1179656 | tf_op jit(solution)/shard_map/ppermute | solution.py:270
  77.3 2.2 %copy-start.1 = (bf16[2048,1024]{1,0:T(8,128)(2,1)S(1)}, bf16[2048,1024]{1,0:T(8,128)(2,1)}, u32[]{:S(2)}) copy-start(bf16[2048,1024]{1,0:T(8,128)(2,1)} %own_ref.1) | copy-start | bytes 12582916
  86.5 6.5 %copy-start.3 = (s16[264,768]{1,0:T(8,128)(2,1)}, s16[264,768]{1,0:T(8,128)(2,1)S(1)}, u32[]{:S(2)}) copy-start(s16[264,768]{1,0:T(8,128)(2,1)S(1)} %get-tuple-element.23.refs_5_) | copy-start | bytes 1216516
  86.6 6.5 %copy-start.4 = (s16[264,768]{1,0:T(8,128)(2,1)}, s16[264,768]{1,0:T(8,128)(2,1)S(1)}, u32[]{:S(2)}) copy-start(s16[264,768]{1,0:T(8,128)(2,1)S(1)} %get-tuple-element.22.refs_6_) | copy-start | bytes 1216516
  86.6 6.5 %copy-start.5 = (s16[264,768]{1,0:T(8,128)(2,1)}, s16[264,768]{1,0:T(8,128)(2,1)S(1)}, u32[]{:S(2)}) copy-start(s16[264,768]{1,0:T(8,128)(2,1)S(1)} %get-tuple-element.24.refs_7_) | copy-start | bytes 1216516
  93.0 6.2 %copy-start.6 = (s16[264,768]{1,0:T(8,128)(2,1)}, s16[264,768]{1,0:T(8,128)(2,1)S(1)}, u32[]{:S(2)}) copy-start(s16[264,768]{1,0:T(8,128)(2,1)S(1)} %get-tuple-element.28.refs_3_) | copy-start | bytes 1216516
  93.0 6.2 %copy-start.7 = (s16[264,768]{1,0:T(8,128)(2,1)}, s16[264,768]{1,0:T(8,128)(2,1)S(1)}, u32[]{:S(2)}) copy-start(s16[264,768]{1,0:T(8,128)(2,1)S(1)} %get-tuple-element.27.refs_1_) | copy-start | bytes 1216516
  99.2 18.5 %all-to-all-start.2 = ((s16[64,8,512]{2,1,0:T(8,128)(2,1)}), s16[64,8,512]{2,1,0:T(8,128)(2,1)S(1)}, u32[]{:S(2)}, u32[]{:S(2)}) async-start(s16[64,8,512]{2,1,0:T(8,128)(2,1)} %bitcast.9), calls=%async_computation.2 | async-start | bytes 1048576 | tf_op jit(solution)/shard_map/all_to_all | solution.py:428
  108.9 32.7 %collective-permute-start.11 = (s16[264,768]{1,0:T(8,128)(2,1)}, s16[264,768]{1,0:T(8,128)(2,1)S(1)}, u32[]{:S(2)}, u32[]{:S(2)}) collective-permute-start(s16[264,768]{1,0:T(8,128)(2,1)} %get-tuple-element.25.refs_2_), channel_id=1, source_target_pairs={{0,4},{2,6},{4,0},{6,2},{8,12},{10,14},{12,8},{14,10},{1,5},{3,7},... | collective-permute-start | bytes 1216520 | tf_op jit(solution)/shard_map/ppermute | solution.py:409
  110.8 31.3 %collective-permute-start.12 = (s16[264,768]{1,0:T(8,128)(2,1)}, s16[264,768]{1,0:T(8,128)(2,1)}, u32[]{:S(2)}, u32[]{:S(2)}) collective-permute-start(s16[264,768]{1,0:T(8,128)(2,1)} %get-tuple-element.26.refs_4_), channel_id=1, source_target_pairs={{0,8},{2,10},{4,12},{6,14},{8,0},{10,2},{12,4},{14,6},{1,9},{3,11}... | collective-permute-start | bytes 1216520 | tf_op jit(solution)/shard_map/ppermute | solution.py:409
  118.1 1.0 copy-start.2
  119.1 81.7 %all-to-all-start.3 = ((s16[128,8,512]{2,1,0:T(8,128)(2,1)}), s16[128,8,512]{2,1,0:T(8,128)(2,1)S(1)}, u32[]{:S(2)}, u32[]{:S(2)}) async-start(s16[128,8,512]{2,1,0:T(8,128)(2,1)} %copy-done.2), calls=%async_computation.3 | async-start | bytes 2097152 | tf_op jit(solution)/shard_map/all_to_all | solution.py:445
  135.8 20.4 %collective-permute-start.13 = (s16[264,768]{1,0:T(8,128)(2,1)}, s16[264,768]{1,0:T(8,128)(2,1)S(1)}, u32[]{:S(2)}, u32[]{:S(2)}) collective-permute-start(s16[264,768]{1,0:T(8,128)(2,1)} %copy-done.7), channel_id=1, source_target_pairs={{0,2},{2,4},{4,6},{6,0},{8,10},{10,12},{12,14},{14,8},{1,3},{3,5},... | collective-permute-start | bytes 1216520 | tf_op jit(solution)/shard_map/ppermute | solution.py:409
  137.1 20.0 %collective-permute-start.14 = (s16[264,768]{1,0:T(8,128)(2,1)}, s16[264,768]{1,0:T(8,128)(2,1)S(1)}, u32[]{:S(2)}, u32[]{:S(2)}) collective-permute-start(s16[264,768]{1,0:T(8,128)(2,1)} %copy-done.6), channel_id=1, source_target_pairs={{0,6},{2,0},{4,2},{6,4},{8,14},{10,8},{12,10},{14,12},{1,7},{3,1},... | collective-permute-start | bytes 1216520 | tf_op jit(solution)/shard_map/ppermute | solution.py:409
  137.3 36.6 %collective-permute-start.10 = (s16[264,768]{1,0:T(8,128)(2,1)}, s16[264,768]{1,0:T(8,128)(2,1)S(1)}, u32[]{:S(2)}, u32[]{:S(2)}) collective-permute-start(s16[264,768]{1,0:T(8,128)(2,1)} %copy-done.5), channel_id=1, source_target_pairs={{0,14},{2,8},{4,10},{6,12},{8,6},{10,0},{12,2},{14,4},{1,15},{3,9}... | collective-permute-start | bytes 1216520 | tf_op jit(solution)/shard_map/ppermute | solution.py:409
  141.6 51.9 %collective-permute-start.8 = (s16[264,768]{1,0:T(8,128)(2,1)}, s16[264,768]{1,0:T(8,128)(2,1)S(1)}, u32[]{:S(2)}, u32[]{:S(2)}) collective-permute-start(s16[264,768]{1,0:T(8,128)(2,1)} %copy-done.4), channel_id=1, source_target_pairs={{0,12},{2,14},{4,8},{6,10},{8,4},{10,6},{12,0},{14,2},{1,13},{3,15... | collective-permute-start | bytes 1216520 | tf_op jit(solution)/shard_map/ppermute | solution.py:409
  142.1 51.4 %collective-permute-start.9 = (s16[264,768]{1,0:T(8,128)(2,1)}, s16[264,768]{1,0:T(8,128)(2,1)S(1)}, u32[]{:S(2)}, u32[]{:S(2)}) collective-permute-start(s16[264,768]{1,0:T(8,128)(2,1)} %copy-done.3), channel_id=1, source_target_pairs={{0,10},{2,12},{4,14},{6,8},{8,2},{10,4},{12,6},{14,0},{1,11},{3,13... | collective-permute-start | bytes 1216520 | tf_op jit(solution)/shard_map/ppermute | solution.py:409
  196.1 0.7 copy-start.9
  196.8 2.1 %collective-permute-start.15 = (bf16[128,768]{1,0:T(8,128)(2,1)}, bf16[128,768]{1,0:T(8,128)(2,1)S(1)}, u32[]{:S(2)}, u32[]{:S(2)}) collective-permute-start(bf16[128,768]{1,0:T(8,128)(2,1)} %get-tuple-element.30), channel_id=1, source_target_pairs={{0,1},{1,0},{2,3},{3,2},{4,5},{5,4},{6,7},{7,6},{8,9},{9,8},{10,11... | collective-permute-start | bytes 589832 | tf_op jit(solution)/shard_map/ppermute | solution.py:420
